TPU v7x, 32 devices: a whole 2x2x4 slice. The times are simulated.
32 devices in a mesh: row: 4 (over x, core), col: 4 (over z), pt: 2 (over y).
Axes of the slice: x: 2, y: 2, z: 4, core: 2. Of those that a mesh axis runs over, the one named last changes fastest.
Arguments:
- first_factors: int32 [32, 1024, 1024], P('pt', 'row', 'col'), may hold values from 0 to 12288
- second_factors: int32 [32, 1024, 1024], P('pt', 'row', 'col'), may hold values from 0 to 12288
Outputs:
- scaled_product: float32 [45, 1024, 1024], P(None, ('row', 'pt'), 'col')
All inputs are finite; a program needn't handle non-finite values.
Results may differ from a plain program's by a relative error of at most 0.0003.
Values may be sent and summed in bfloat16 or wider, within the bound.
A program may use at most 128 MiB of HBM per device.

v0:
```python
import jax
import jax.numpy as jnp
import numpy as np
from jax import lax
from jax.sharding import PartitionSpec as P

DEG = 16


modulus = 12289
digit_base = 128


def primitive_root():
    for candidate in range(2, modulus):
        if pow(candidate, 6144, modulus) != 1 and pow(candidate, 4096, modulus) != 1:
            return candidate
    return 0


def make_table(order_size, row_count, column_count, inverse):
    generator = primitive_root()
    root_value = pow(generator, (modulus - 1) // order_size, modulus)
    scaling = 1
    if inverse:
        root_value = pow(root_value, modulus - 2, modulus)
        scaling = pow(order_size, modulus - 2, modulus)
    entries = [
        [
            pow(root_value, row_index * column_index % order_size, modulus) * scaling % modulus
            for column_index in range(column_count)
        ]
        for row_index in range(row_count)
    ]
    return np.array(entries, dtype=np.int64)


def value_digits(values):
    high_digit = values // digit_base
    return (
        high_digit.astype(jnp.bfloat16),
        (values - digit_base * high_digit).astype(jnp.bfloat16),
    )


def combine(high_high, high_low, low_high, low_low):
    top_part = high_high.astype(jnp.int32) % modulus
    middle_part = (high_low.astype(jnp.int32) + low_high.astype(jnp.int32)) % modulus
    return (
        top_part * (digit_base * digit_base) % modulus
        + middle_part * digit_base
        + low_low.astype(jnp.int32)
    ) % modulus


def transform(matrix_table, coefs):
    slot_count = coefs.shape[0]
    flat_coefs = coefs.reshape(slot_count, -1)
    table_high = jnp.asarray(matrix_table // digit_base, dtype=jnp.bfloat16)
    table_low = jnp.asarray(matrix_table % digit_base, dtype=jnp.bfloat16)
    data_high, data_low = value_digits(flat_coefs)

    def product_of(left_part, right_part):
        return jnp.dot(left_part, right_part, preferred_element_type=jnp.float32)

    mixed_values = combine(
        product_of(table_high, data_high),
        product_of(table_high, data_low),
        product_of(table_low, data_high),
        product_of(table_low, data_low),
    )
    return mixed_values.reshape(matrix_table.shape[0], coefs.shape[1], coefs.shape[2])


def batched_product(left_part, right_part):
    return jnp.einsum("bik,bkj->bij", left_part, right_part, preferred_element_type=jnp.float32)


def digit_sum(totals, left_digits, right_digits):
    return (
        totals[0] + batched_product(left_digits[0], right_digits[0]),
        totals[1] + batched_product(left_digits[0], right_digits[1]),
        totals[2] + batched_product(left_digits[1], right_digits[0]),
        totals[3] + batched_product(left_digits[1], right_digits[1]),
    )


def pointwise(left_values, right_values):
    left_points, right_points = (
        lax.all_to_all(
            lax.all_to_all(
                left_values.astype(jnp.float32), "col", split_axis=0, concat_axis=2, tiled=True
            ),
            "pt",
            split_axis=0,
            concat_axis=1,
            tiled=True,
        ),
        lax.all_to_all(
            lax.all_to_all(
                right_values.astype(jnp.float32), "col", split_axis=0, concat_axis=2, tiled=True
            ),
            "pt",
            split_axis=0,
            concat_axis=1,
            tiled=True,
        ),
    )
    left_digits = value_digits(left_points.astype(jnp.int32))
    right_digits = value_digits(right_points.astype(jnp.int32))
    zeros_init = jnp.zeros(left_points.shape, jnp.float32)
    column_parts = tuple((digit_part for digit_part in left_digits))
    totals = digit_sum(
        (zeros_init, zeros_init, zeros_init, zeros_init),
        column_parts,
        (
            lax.all_gather(right_digits[0], "row", axis=1, tiled=True),
            lax.all_gather(right_digits[1], "row", axis=1, tiled=True),
        ),
    )
    product_values = combine(totals[0], totals[1], totals[2], totals[3]).astype(jnp.float32)
    arrived = lax.all_to_all(
        lax.all_to_all(product_values, "col", split_axis=2, concat_axis=0, tiled=True),
        "pt",
        split_axis=1,
        concat_axis=0,
        tiled=True,
    )
    col_count = lax.axis_size("col")
    pt_count = lax.axis_size("pt")
    local_count = arrived.shape[0] // (col_count * pt_count)
    returned = arrived.reshape(pt_count, col_count, local_count, arrived.shape[1], arrived.shape[2])
    returned = returned.transpose(1, 0, 2, 3, 4).reshape(arrived.shape)
    return returned.astype(jnp.int32)


def local(first_factors, second_factors):
    forward_one = make_table(2 * DEG, 2 * DEG, DEG, False)
    inverse_one = make_table(2 * DEG, 2 * DEG, 2 * DEG, True)
    forward_two = make_table(4 * DEG, 4 * DEG, 2 * DEG, False)
    inverse_two = make_table(4 * DEG, 3 * DEG - 3, 4 * DEG, True)
    first_entries, second_entries = (
        lax.all_to_all(
            first_factors.astype(jnp.float32), "pt", split_axis=1, concat_axis=0, tiled=True
        ),
        lax.all_to_all(
            second_factors.astype(jnp.float32), "pt", split_axis=1, concat_axis=0, tiled=True
        ),
    )
    first_entries = first_entries.astype(jnp.int32)
    second_entries = second_entries.astype(jnp.int32)
    left_values = jnp.concatenate(
        [transform(forward_one, first_entries[:DEG]), transform(forward_one, first_entries[DEG:])],
        0,
    )
    right_values = jnp.concatenate(
        [
            transform(forward_one, second_entries[:DEG]),
            transform(forward_one, second_entries[DEG:]),
        ],
        0,
    )
    products = pointwise(left_values, right_values)
    first_product = transform(inverse_one, products[: 2 * DEG])
    second_product = transform(inverse_one, products[2 * DEG :])
    upper_values = transform(forward_two, first_product)
    lower_values = transform(forward_two[:, :DEG], second_product[DEG:])
    result_coefficients = transform(inverse_two, pointwise(upper_values, lower_values))
    return result_coefficients.astype(jnp.float32) / 12289.0


def solution(mesh):
    in_specs = (P("pt", "row", "col"), P("pt", "row", "col"))
    out_specs = P(None, ("row", "pt"), "col")
    return jax.shard_map(local, mesh=mesh, in_specs=in_specs, out_specs=out_specs, check_vma=False)
```

profile of v0, /device:TPU:0, one launch (start us, length us, event | category | flops | bytes accessed | tf_op | source)
XLA Modules:
  0.0 2418.5 jit_solution(8705396629811589030)
XLA Ops:
  6.5 4.6 copy_convert_fusion.2
  11.2 51.9 %all_to_all.186 = f32[16,256,256]{2,0,1:T(8,128)S(1)} all-to-all(f32[16,256,256]{2,0,1:T(8,128)S(1)} %copy_convert_fusion.2), channel_id=1, replica_groups=mesh['row'=4,'col'=4,'pt'=2] {'pt'}, dimensions={1} | all-to-all | bytes 8388608 | tf_op jit(solution)/shard_map/all_to_all | solution.py:146
  81.8 8.7 add_select_fusion.35
  95.0 8.2 add_select_fusion.39
  109.7 187.2 %all_to_all.187 = f32[64,128,256]{2,1,0:T(8,128)} all-to-all(f32[64,128,256]{2,1,0:T(8,128)S(1)} %add_convert_fusion.1), channel_id=1, replica_groups=mesh['row'=4,'col'=4,'pt'=2] {'col'}, dimensions={0} | all-to-all | bytes 16777216 | tf_op jit(solution)/shard_map/all_to_all | solution.py:100
  296.8 9.2 copy.91
  306.1 96.0 %all_to_all.188 = f32[16,128,1024]{1,2,0:T(8,128)S(1)} all-to-all(f32[16,128,1024]{1,2,0:T(8,128)} %bitcast.345), channel_id=1, replica_groups=mesh['row'=4,'col'=4,'pt'=2] {'pt'}, dimensions={0} | all-to-all | bytes 16777216 | tf_op jit(solution)/shard_map/all_to_all | solution.py:99
  406.1 9.2 copy.93
  415.2 10.2 fusion.104
  425.5 4.6 copy_convert_fusion.3
  430.1 48.3 %all_to_all.189 = f32[16,256,256]{2,0,1:T(8,128)S(1)} all-to-all(f32[16,256,256]{2,0,1:T(8,128)S(1)} %copy_convert_fusion.3), channel_id=1, replica_groups=mesh['row'=4,'col'=4,'pt'=2] {'pt'}, dimensions={1} | all-to-all | bytes 8388608 | tf_op jit(solution)/shard_map/all_to_all | solution.py:143
  493.6 9.7 add_select_fusion.43
  513.8 8.2 add_select_fusion.47
  528.5 184.9 %all_to_all.190 = f32[64,128,256]{2,1,0:T(8,128)} all-to-all(f32[64,128,256]{2,1,0:T(8,128)S(1)} %add_convert_fusion), channel_id=1, replica_groups=mesh['row'=4,'col'=4,'pt'=2] {'col'}, dimensions={0} | all-to-all | bytes 16777216 | tf_op jit(solution)/shard_map/all_to_all | solution.py:91
  713.4 9.3 copy.86
  722.7 95.7 %all_to_all.191 = f32[16,128,1024]{1,2,0:T(8,128)S(1)} all-to-all(f32[16,128,1024]{1,2,0:T(8,128)} %bitcast.348), channel_id=1, replica_groups=mesh['row'=4,'col'=4,'pt'=2] {'pt'}, dimensions={0} | all-to-all | bytes 16777216 | tf_op jit(solution)/shard_map/all_to_all | solution.py:90
  822.4 9.2 copy.88
  831.6 10.2 fusion.118
  841.8 14.9 fusion.192
  856.7 9.4 fusion.190
  866.1 14.9 fusion.191
  881.1 27.7 %fusion.78 = f32[8,256,1024]{2,1,0:T(8,128)} fusion(f32[8,256,1024]{2,1,0:T(8,128)} %fusion.192, f32[8,256,1024]{2,1,0:T(8,128)} %fusion.191, f32[8,256,1024]{2,1,0:T(8,128)} %fusion.190, bf16[8,256,1024]{2,1,0:T(8,128)(2,1)} %get-tuple-element.16, bf16[8,1024,1024]{2,1,0:T(8,128)(2,1)S(1)} %copy-done.2), kind=kOutput, calls=%fused_computation.154 | convolution fusion | flops 4366270464 | bytes 54525952 | tf_op jit(solution)/shard_map/bik,bkj->bij/dot_general | solution.py:76
  908.7 9.3 copy.94
  918.0 188.0 %all_to_all.192 = f32[8,256,1024]{1,0,2:T(8,128)} all-to-all(f32[8,256,1024]{1,0,2:T(8,128)} %copy.94), channel_id=1, replica_groups=mesh['row'=4,'col'=4,'pt'=2] {'col'}, dimensions={2} | all-to-all | bytes 16777216 | tf_op jit(solution)/shard_map/all_to_all | solution.py:123
  1106.0 9.9 copy.96
  1115.9 8.2 copy.97
  1124.2 93.8 %all_to_all.193 = f32[32,256,256]{2,0,1:T(8,128)S(1)} all-to-all(f32[32,256,256]{2,0,1:T(8,128)S(1)} %copy.97), channel_id=1, replica_groups=mesh['row'=4,'col'=4,'pt'=2] {'pt'}, dimensions={1} | all-to-all | bytes 16777216 | tf_op jit(solution)/shard_map/all_to_all | solution.py:122
  1218.0 8.1 copy_convert_fusion.1
  1238.1 8.1 add_select_fusion.26
  1247.7 5.6 fusion.148
  1261.7 4.7 fusion.5
  1266.4 15.0 fusion.89
  1283.9 184.5 %all_to_all.194 = f32[64,128,256]{2,1,0:T(8,128)} all-to-all(f32[64,128,256]{2,1,0:T(8,128)S(1)} %bitcast.353), channel_id=1, replica_groups=mesh['row'=4,'col'=4,'pt'=2] {'col'}, dimensions={0} | all-to-all | bytes 16777216 | tf_op jit(solution)/shard_map/all_to_all | solution.py:100
  1468.4 9.2 copy.105
  1477.6 95.4 %all_to_all.195 = f32[16,128,1024]{1,2,0:T(8,128)S(1)} all-to-all(f32[16,128,1024]{1,2,0:T(8,128)} %bitcast.355), channel_id=1, replica_groups=mesh['row'=4,'col'=4,'pt'=2] {'pt'}, dimensions={0} | all-to-all | bytes 16777216 | tf_op jit(solution)/shard_map/all_to_all | solution.py:99
  1577.1 9.2 copy.107
  1586.2 10.2 fusion.100
  1596.5 4.6 copy.100
  1601.1 4.9 fusion.32
  1609.6 4.8 fusion.66
  1614.4 9.8 add_select_fusion.30
  1628.5 7.7 fusion.13
  1636.2 10.1 fusion.15
  1646.3 17.2 fusion.83
  1666.0 184.4 %all_to_all.196 = f32[64,128,256]{2,1,0:T(8,128)} all-to-all(f32[64,128,256]{2,1,0:T(8,128)S(1)} %bitcast.357), channel_id=1, replica_groups=mesh['row'=4,'col'=4,'pt'=2] {'col'}, dimensions={0} | all-to-all | bytes 16777216 | tf_op jit(solution)/shard_map/all_to_all | solution.py:91
  1850.5 9.3 copy.101
  1859.8 95.6 %all_to_all.197 = f32[16,128,1024]{1,2,0:T(8,128)S(1)} all-to-all(f32[16,128,1024]{1,2,0:T(8,128)} %bitcast.359), channel_id=1, replica_groups=mesh['row'=4,'col'=4,'pt'=2] {'pt'}, dimensions={0} | all-to-all | bytes 16777216 | tf_op jit(solution)/shard_map/all_to_all | solution.py:90
  1959.4 9.2 copy.103
  1968.6 10.2 fusion.120
  1978.8 14.9 fusion.195
  1993.7 9.4 fusion.193
  2003.1 14.9 fusion.194
  2018.0 27.7 %fusion.97 = f32[8,256,1024]{2,1,0:T(8,128)} fusion(f32[8,256,1024]{2,1,0:T(8,128)} %fusion.195, f32[8,256,1024]{2,1,0:T(8,128)} %fusion.194, f32[8,256,1024]{2,1,0:T(8,128)} %fusion.193, bf16[8,256,1024]{2,1,0:T(8,128)(2,1)} %get-tuple-element.10, bf16[8,1024,1024]{2,1,0:T(8,128)(2,1)S(1)} %copy-done.3), kind=kOutput, calls=%fused_computation.173 | convolution fusion | flops 4366270464 | bytes 54525952 | tf_op jit(solution)/shard_map/bik,bkj->bij/dot_general | solution.py:76
  2045.7 9.3 copy.108
  2055.0 187.9 %all_to_all.198 = f32[8,256,1024]{1,0,2:T(8,128)} all-to-all(f32[8,256,1024]{1,0,2:T(8,128)} %copy.108), channel_id=1, replica_groups=mesh['row'=4,'col'=4,'pt'=2] {'col'}, dimensions={2} | all-to-all | bytes 16777216 | tf_op jit(solution)/shard_map/all_to_all | solution.py:123
  2242.9 9.9 copy.110
  2252.8 8.2 copy.111
  2261.1 93.8 %all_to_all.199 = f32[32,256,256]{2,0,1:T(8,128)S(1)} all-to-all(f32[32,256,256]{2,0,1:T(8,128)S(1)} %copy.111), channel_id=1, replica_groups=mesh['row'=4,'col'=4,'pt'=2] {'pt'}, dimensions={1} | all-to-all | bytes 16777216 | tf_op jit(solution)/shard_map/all_to_all | solution.py:122
  2354.9 4.9 copy_convert_fusion
  2359.8 4.7 copy.114
  2364.5 6.9 convolution_convert_fusion.10
  2371.4 8.5 fusion.23
  2380.0 9.2 fusion.21
  2389.2 17.2 fusion.117
  (95 shorter events, 117.9 us)
Async XLA Ops:
  6.5 835.2 %all-gather.5.cloned.1.call-start = ((), (), s32[]{:S(2)}) async-start(), calls=%async_computation.14 | async-start | bytes 20971520 | tf_op jit(solution)/shard_map/all_gather | solution.py:117
  66.4 1.2 copy-start.14
  75.5 3.1 copy-start.13
  425.4 440.7 %all-gather.7.cloned.1.call-start = ((), (), s32[]{:S(2)}) async-start(), calls=%async_computation.15 | async-start | bytes 20971520 | tf_op jit(solution)/shard_map/all_gather | solution.py:118
  483.1 6.1 copy-start.4
  493.5 1485.3 %all-gather.9.cloned.1.call-start = ((), (), s32[]{:S(2)}) async-start(), calls=%async_computation.16 | async-start | bytes 20971520 | tf_op jit(solution)/shard_map/all_gather | solution.py:117
  841.8 15.0 copy-start
  866.1 14.9 copy-start.2
  1235.3 2.8 copy-start.8
  1246.2 0.7 copy-start.7
  1253.3 2.8 copy-start.5
  1260.5 1.2 copy-start.6
  1596.4 406.7 %all-gather.11.cloned.1.call-start = ((), (), s32[]{:S(2)}) async-start(), calls=%async_computation.17 | async-start | bytes 20971520 | tf_op jit(solution)/shard_map/all_gather | solution.py:118
  1614.4 9.8 copy-start.10
  1624.2 4.3 copy-start.16
  1624.2 4.3 copy-start.9
  1636.2 10.1 copy-start.15
  1636.2 10.1 copy-start.17
  1978.8 15.0 copy-start.1
  2003.1 14.9 copy-start.3
  2359.8 4.8 copy-start.12
  2371.4 8.6 copy-start.11
Sparse Core Ops, SparseCore 0:
  425.5 104.7 all-gather.4
  531.9 105.8 all-gather.6
  1596.5 104.9 all-gather.8
  1702.9 105.8 all-gather.10
where the time goes:
time: 2420 us
  blocking collectives  1790 us (74%)
  matrix products  347 us (14%)
  local copies, waits for them, and re-layouts  177 us (7%)
  other arithmetic  92.1 us (4%)
    all_to_all x2, blocking collectives, pointwise(): lax.all_to_all(product_values, 'col', split_axis=2, concat_axis=0, tiled=...  376 us
    all_to_all x2, blocking collectives, pointwise(): lax.all_to_all(right_values.astype(jnp.float32), 'col', split_axis=0, con...  372 us
    all_to_all x2, blocking collectives, pointwise(): lax.all_to_all(left_values.astype(jnp.float32), 'col', split_axis=0, conc...  369 us
    dot_general x36, matrix products, product_of(): return jnp.dot(left_part, right_part, preferred_element_type=jnp.float32)  214 us
    all_to_all x2, blocking collectives, pointwise(): lax.all_to_all(lax.all_to_all(left_values.astype(jnp.float32), 'col', spl...  191 us
    all_to_all x2, blocking collectives, pointwise(): lax.all_to_all(lax.all_to_all(right_values.astype(jnp.float32), 'col', sp...  191 us
    all_to_all x2, blocking collectives, pointwise(): lax.all_to_all(lax.all_to_all(product_values, 'col', split_axis=2, concat...  188 us
    dot_general x8, matrix products, batched_product(): jnp.einsum('bik,bkj->bij', left_part, right_part, preferred_element_type=...  134 us
  transfers between devices with their start and end apart: 4, of which 0 were waited for; matrix products, arithmetic and copies ran while one was open for 10% of the time, Pallas kernels for 0%

commit v1 on v0

--- a/solution.py
+++ b/solution.py
@@ -169,7 +169,96 @@
     return result_coefficients.astype(jnp.float32) / 12289.0
 
 
+def reduce_centred(values):
+    return values - 12289.0 * jnp.round(values * (1.0 / 12289.0))
+
+
+def centred_digits(values):
+    high_digit = jnp.round(values * (1.0 / 128.0))
+    return high_digit.astype(jnp.bfloat16), (values - 128.0 * high_digit).astype(jnp.bfloat16)
+
+
+def combine_centred(high_high, middle, low_low):
+    upper_part = reduce_centred(reduce_centred(high_high) * 128.0 + middle)
+    return reduce_centred(upper_part * 128.0 + low_low)
+
+
+def table_digits(matrix_table):
+    centred = np.where(matrix_table > modulus // 2, matrix_table - modulus, matrix_table)
+    high_digit = np.round(centred / 128.0)
+    return high_digit, centred - 128.0 * high_digit
+
+
+def centred_transform(table_high, table_low, coefs):
+    data_high, data_low = centred_digits(coefs.astype(jnp.float32))
+    table_high = jnp.asarray(table_high, dtype=jnp.bfloat16)
+    table_low = jnp.asarray(table_low, dtype=jnp.bfloat16)
+
+    def product_of(left_part, right_part):
+        return jnp.einsum("ts,sab->tab", left_part, right_part, preferred_element_type=jnp.float32)
+
+    middle = product_of(
+        jnp.concatenate([table_high, table_low], 1), jnp.concatenate([data_low, data_high], 0)
+    )
+    return combine_centred(
+        product_of(table_high, data_high), middle, product_of(table_low, data_low)
+    )
+
+
+def column_pointwise(left_values, right_values):
+    right_points = lax.all_to_all(
+        right_values.astype(jnp.int16), "col", split_axis=0, concat_axis=2, tiled=True
+    )
+    right_points = lax.all_gather(right_points, "row", axis=1, tiled=True)
+    left_points = lax.all_to_all(
+        left_values.astype(jnp.int16), "col", split_axis=0, concat_axis=2, tiled=True
+    )
+    left_high, left_low = centred_digits(left_points.astype(jnp.float32))
+    right_high, right_low = centred_digits(right_points.astype(jnp.float32))
+    middle = batched_product(left_high, right_low) + batched_product(left_low, right_high)
+    product_values = combine_centred(
+        batched_product(left_high, right_high), middle, batched_product(left_low, right_low)
+    )
+    return lax.all_to_all(
+        product_values.astype(jnp.int16), "col", split_axis=2, concat_axis=0, tiled=True
+    )
+
+
+def pair_local(first_factors, second_factors):
+    forward_one = table_digits(make_table(2 * DEG, 2 * DEG, DEG, False))
+    inverse_one = table_digits(make_table(2 * DEG, 2 * DEG, 2 * DEG, True))
+    forward_two = table_digits(make_table(4 * DEG, 4 * DEG, 2 * DEG, False))
+    inverse_two = table_digits(make_table(4 * DEG, 3 * DEG - 3, 4 * DEG, True))
+    half_points = 2 * DEG
+    place = lax.axis_index("pt")
+    products = column_pointwise(
+        centred_transform(*forward_one, centre(first_factors)),
+        centred_transform(*forward_one, centre(second_factors)),
+    )
+    own_product = centred_transform(*inverse_one, products).astype(jnp.int16)
+    both_products = lax.all_gather(own_product, "pt", axis=0, tiled=True)
+    first_product = both_products[: 2 * DEG]
+    shifted = both_products[3 * DEG :]
+    own_tables = [
+        lax.dynamic_slice_in_dim(
+            jnp.asarray(digit, dtype=jnp.bfloat16), place * half_points, half_points, 0
+        )
+        for digit in forward_two
+    ]
+    upper_values = centred_transform(*own_tables, first_product)
+    lower_values = centred_transform(*[digit[:, :DEG] for digit in own_tables], shifted)
+    products_two = column_pointwise(upper_values, lower_values)
+    all_points = lax.all_to_all(products_two, "pt", split_axis=1, concat_axis=0, tiled=True)
+    result = centred_transform(*inverse_two, all_points)
+    return jnp.where(result < 0.0, result + 12289.0, result) / 12289.0
+
+
+def centre(values):
+    return jnp.where(values > modulus // 2, values - modulus, values)
+
+
 def solution(mesh):
     in_specs = (P("pt", "row", "col"), P("pt", "row", "col"))
     out_specs = P(None, ("row", "pt"), "col")
-    return jax.shard_map(local, mesh=mesh, in_specs=in_specs, out_specs=out_specs, check_vma=False)
+    body = pair_local if mesh.shape["pt"] == 2 else local
+    return jax.shard_map(body, mesh=mesh, in_specs=in_specs, out_specs=out_specs, check_vma=False)

time: 2420 us -> 1270 us (0.52)
  blocking collectives: 1790 us -> 452 us
  waiting for transfers between devices: 0.11 us -> 364 us
  matrix products: 347 us -> 221 us
  other arithmetic: 92.1 us -> 45.2 us
  local copies, waits for them, and re-layouts: 177 us -> 148 us
  starting transfers between devices: 0.13 us -> 27.2 us
    all_to_all x14 -> x2, blocking collectives: 1790 us -> 150 us  [the longest x1 99.7 us: column_pointwise(): lax.all_to_all(product_values.astype(jnp.int16), 'col', split_axis=2, con...]
    all_to_all x0 -> x5, waiting for transfers between devices: none -> 364 us  [the longest x2 144 us: column_pointwise(): lax.all_to_all(left_values.astype(jnp.int16), 'col', split_axis=0, concat...]
    all_gather x0 -> x3, blocking collectives: none -> 303 us  [the longest x2 210 us: column_pointwise(): right_points = lax.all_gather(right_points, 'row', axis=1, tiled=True)]
    dot_general x36 -> x18, matrix products: 214 us -> 65.3 us  [product_of(): jnp.einsum('ts,sab->tab', left_part, right_part, preferred_element_type=j...]
    convert_element_type x18 -> x10, other arithmetic: 92.1 us -> 45.2 us  [the longest x3 15.4 us: centred_digits(): high_digit.astype(jnp.bfloat16)]
    all_to_all x8 -> x7, local copies, waits for them, and re-layouts: 73.4 us -> 45.5 us  [the longest x4 30.7 us: column_pointwise(): lax.all_to_all(right_values.astype(jnp.int16), 'col', split_axis=0, conca...]
    all_to_all x0 -> x5, starting transfers between devices: none -> 27.2 us  [the longest x2 11.7 us: column_pointwise(): lax.all_to_all(left_values.astype(jnp.int16), 'col', split_axis=0, concat...]
    convert_element_type x10 -> x12, local copies, waits for them, and re-layouts: 68.7 us -> 95.2 us  [the longest x4 45.7 us: column_pointwise(): left_high, left_low = centred_digits(left_points.astype(jnp.float32))]
  transfers between devices with their start and end apart: 4 -> 5, of which waited for: 0 -> 5; matrix products, arithmetic and copies ran while one was open for 10% -> 8% of each run, Pallas kernels for 0% -> 0%
where the time goes in v1:
time: 1270 us; the launch traced here: 1260 us
  blocking collectives  452 us (36%)
  waiting for transfers between devices  364 us (29%)
  matrix products  221 us (17%)
  local copies, waits for them, and re-layouts  148 us (12%)
  other arithmetic  45.2 us (4%)
  starting transfers between devices  27.2 us (2%)
    all_gather x2, blocking collectives, column_pointwise(): right_points = lax.all_gather(right_points, 'row', axis=1, tiled=True)  210 us
    dot_general x8, matrix products, batched_product(): jnp.einsum('bik,bkj->bij', left_part, right_part, preferred_element_type=...  156 us
    all_to_all x2, waiting for transfers between devices, column_pointwise(): lax.all_to_all(left_values.astype(jnp.int16), 'col', split_axis=0, concat...  144 us
    all_to_all x2, waiting for transfers between devices, column_pointwise(): lax.all_to_all(right_values.astype(jnp.int16), 'col', split_axis=0, conca...  126 us
    all_to_all x1, blocking collectives, column_pointwise(): lax.all_to_all(product_values.astype(jnp.int16), 'col', split_axis=2, con...  99.7 us
    all_to_all x1, waiting for transfers between devices, column_pointwise(): lax.all_to_all(product_values.astype(jnp.int16), 'col', split_axis=2, con...  94 us
    all_gather x1, blocking collectives, pair_local(): both_products = lax.all_gather(own_product, 'pt', axis=0, tiled=True)  92.8 us
    dot_general x18, matrix products, product_of(): jnp.einsum('ts,sab->tab', left_part, right_part, preferred_element_type=j...  65.3 us
  transfers between devices with their start and end apart: 5, of which 5 were waited for; matrix products, arithmetic and copies ran while one was open for 8% of the time, Pallas kernels for 0%

profile of v1, /device:TPU:0, one launch (start us, length us, event | category | flops | bytes accessed | tf_op | source)
XLA Modules:
  0.0 1258.8 jit_solution(4259190581243966023)
XLA Ops:
  0.0 5.5 fusion.68
  6.8 1.4 fusion.55
  8.2 7.1 subtract_convert_fusion.8
  15.3 4.3 copy.69
  19.6 6.6 all-to-all-start
  26.2 5.4 fusion.67
  31.7 1.4 fusion.59
  34.3 7.1 subtract_convert_fusion.7
  41.4 4.4 copy.74
  45.8 73.8 %all-to-all-done = s16[32,256,256]{2,1,0:T(8,128)(2,1)} async-done(((s16[32,256,256]{2,1,0:T(8,128)(2,1)}), s16[32,256,256]{2,1,0:T(8,128)(2,1)}, u32[]{:S(2)}, u32[]{:S(2)}) %all-to-all-start) | async-done | bytes 4194336 | tf_op jit(solution)/shard_map/all_to_all | solution.py:213
  119.6 5.3 all-to-all-start.1
  124.9 6.8 convert.12
  131.8 12.0 copy.111
  143.8 10.8 reshape.16
  154.6 63.0 %all-to-all-done.1 = s16[32,256,256]{2,1,0:T(8,128)(2,1)} async-done(((s16[32,256,256]{2,1,0:T(8,128)(2,1)}), s16[32,256,256]{2,1,0:T(8,128)(2,1)}, u32[]{:S(2)}, u32[]{:S(2)}) %all-to-all-start.1) | async-done | bytes 4194336 | tf_op jit(solution)/shard_map/all_to_all | solution.py:209
  217.6 7.4 copy.113
  225.0 7.9 all_to_all.71
  232.9 105.4 %all-gather.3 = s16[8,1024,1024]{2,1,0:T(8,128)(2,1)} all-gather(s16[8,256,1024]{2,1,0:T(8,128)(2,1)} %all_to_all.71), channel_id=1, replica_groups=mesh['row'=4,'col'=4,'pt'=2] {'row'}, dimensions={1}, use_global_device_ids=true | all-gather | bytes 20971520 | tf_op jit(solution)/shard_map/all_gather | solution.py:212
  338.4 16.5 %fusion.14 = f32[8,256,1024]{2,1,0:T(8,128)} fusion(s16[8,1024,1024]{2,1,0:T(8,128)(2,1)} %all-gather.3, f32[8,256,1024]{2,1,0:T(8,128)} %reshape.16), kind=kOutput, calls=%fused_computation.16 | convolution fusion | flops 4334813184 | bytes 33554432 | tf_op jit(solution)/shard_map/bik,bkj->bij/dot_general | solution.py:76
  354.9 17.6 %fusion.12 = f32[8,256,1024]{2,1,0:T(8,128)} fusion(s16[8,1024,1024]{2,1,0:T(8,128)(2,1)} %all-gather.3, f32[8,256,1024]{2,1,0:T(8,128)} %reshape.16), kind=kOutput, calls=%fused_computation.15 | convolution fusion | flops 4339007488 | bytes 33554432 | tf_op jit(solution)/shard_map/bik,bkj->bij/dot_general | solution.py:76
  372.5 18.3 %fusion.20 = f32[8,256,1024]{2,1,0:T(8,128)} fusion(s16[8,1024,1024]{2,1,0:T(8,128)(2,1)} %all-gather.3, f32[8,256,1024]{2,1,0:T(8,128)} %reshape.16), kind=kOutput, calls=%fused_computation.23 | convolution fusion | flops 4355784704 | bytes 33554432 | tf_op jit(solution)/shard_map/bik,bkj->bij/dot_general | solution.py:76
  390.8 25.6 %subtract_convert_fusion.5 = s16[8,256,1024]{2,1,0:T(8,128)(2,1)} fusion(f32[8,256,1024]{2,1,0:T(8,128)} %fusion.20, f32[8,256,1024]{2,1,0:T(8,128)} %fusion.12, f32[8,256,1024]{2,1,0:T(8,128)} %fusion.14, s16[8,1024,1024]{2,1,0:T(8,128)(2,1)} %all-gather.3, f32[8,256,1024]{2,1,0:T(8,128)} %reshape.16), kind=kOutput, calls=%fused_computation.59 | convolution fusion | flops 4389339136 | bytes 54525952 | tf_op jit(solution)/shard_map/bik,bkj->bij/dot_general | solution.py:76
  416.3 7.3 copy.76
  423.6 5.1 all-to-all-start.2
  428.8 94.0 %all-to-all-done.2 = s16[8,256,1024]{1,0,2:T(8,128)(2,1)} async-done(((s16[8,256,1024]{1,0,2:T(8,128)(2,1)}), s16[8,256,1024]{1,0,2:T(8,128)(2,1)}, u32[]{:S(2)}, u32[]{:S(2)}) %all-to-all-start.2) | async-done | bytes 4194336 | tf_op jit(solution)/shard_map/all_to_all | solution.py:222
  522.8 6.5 convert.13
  529.3 10.5 copy.77
  539.8 4.5 fusion.46
  545.5 1.5 fusion.28
  547.0 8.1 subtract_convert_fusion.4
  555.1 92.8 %all-gather.4 = s16[64,256,256]{2,0,1:T(8,128)(2,1)S(1)} all-gather(s16[32,256,256]{2,0,1:T(8,128)(2,1)} %subtract_convert_fusion.4), channel_id=1, replica_groups=mesh['row'=4,'col'=4,'pt'=2] {'pt'}, dimensions={0}, use_global_device_ids=true | all-gather | bytes 12582912 | tf_op jit(solution)/shard_map/all_gather | solution.py:239
  648.0 3.1 fusion.27
  651.1 4.6 fusion.84
  657.1 10.0 subtract_convert_fusion.3
  667.0 4.3 copy.78
  671.3 5.1 all-to-all-start.3
  676.4 3.0 fusion.52
  682.9 8.5 subtract_convert_fusion.2
  691.5 6.5 copy.82
  698.0 70.7 %all-to-all-done.3 = s16[32,256,256]{2,1,0:T(8,128)(2,1)} async-done(((s16[32,256,256]{2,1,0:T(8,128)(2,1)}), s16[32,256,256]{2,1,0:T(8,128)(2,1)}, u32[]{:S(2)}, u32[]{:S(2)}) %all-to-all-start.3) | async-done | bytes 4194336 | tf_op jit(solution)/shard_map/all_to_all | solution.py:213
  768.7 5.1 all-to-all-start.4
  773.8 6.8 convert.14
  780.6 12.0 copy.110
  792.6 10.8 reshape.18
  803.4 63.1 %all-to-all-done.4 = s16[32,256,256]{2,1,0:T(8,128)(2,1)} async-done(((s16[32,256,256]{2,1,0:T(8,128)(2,1)}), s16[32,256,256]{2,1,0:T(8,128)(2,1)}, u32[]{:S(2)}, u32[]{:S(2)}) %all-to-all-start.4) | async-done | bytes 4194336 | tf_op jit(solution)/shard_map/all_to_all | solution.py:209
  866.5 7.4 copy.112
  874.0 7.9 all_to_all.77
  881.9 104.5 %all-gather.5 = s16[8,1024,1024]{2,1,0:T(8,128)(2,1)} all-gather(s16[8,256,1024]{2,1,0:T(8,128)(2,1)} %all_to_all.77), channel_id=1, replica_groups=mesh['row'=4,'col'=4,'pt'=2] {'row'}, dimensions={1}, use_global_device_ids=true | all-gather | bytes 20971520 | tf_op jit(solution)/shard_map/all_gather | solution.py:212
  986.4 16.5 %fusion.10 = f32[8,256,1024]{2,1,0:T(8,128)} fusion(s16[8,1024,1024]{2,1,0:T(8,128)(2,1)} %all-gather.5, f32[8,256,1024]{2,1,0:T(8,128)} %reshape.18), kind=kOutput, calls=%fused_computation.14 | convolution fusion | flops 4334813184 | bytes 33554432 | tf_op jit(solution)/shard_map/bik,bkj->bij/dot_general | solution.py:76
  1002.9 17.6 %fusion.8 = f32[8,256,1024]{2,1,0:T(8,128)} fusion(s16[8,1024,1024]{2,1,0:T(8,128)(2,1)} %all-gather.5, f32[8,256,1024]{2,1,0:T(8,128)} %reshape.18), kind=kOutput, calls=%fused_computation.13 | convolution fusion | flops 4339007488 | bytes 33554432 | tf_op jit(solution)/shard_map/bik,bkj->bij/dot_general | solution.py:76
  1020.5 18.3 %fusion.16 = f32[8,256,1024]{2,1,0:T(8,128)} fusion(s16[8,1024,1024]{2,1,0:T(8,128)(2,1)} %all-gather.5, f32[8,256,1024]{2,1,0:T(8,128)} %reshape.18), kind=kOutput, calls=%fused_computation.21 | convolution fusion | flops 4355784704 | bytes 33554432 | tf_op jit(solution)/shard_map/bik,bkj->bij/dot_general | solution.py:76
  1038.7 25.6 %subtract_convert_fusion = s16[8,256,1024]{2,1,0:T(8,128)(2,1)} fusion(f32[8,256,1024]{2,1,0:T(8,128)} %fusion.16, f32[8,256,1024]{2,1,0:T(8,128)} %fusion.8, f32[8,256,1024]{2,1,0:T(8,128)} %fusion.10, s16[8,1024,1024]{2,1,0:T(8,128)(2,1)} %all-gather.5, f32[8,256,1024]{2,1,0:T(8,128)} %reshape.18), kind=kOutput, calls=%fused_computation.52 | convolution fusion | flops 4389339136 | bytes 54525952 | tf_op jit(solution)/shard_map/bik,bkj->bij/dot_general | solution.py:76
  1064.3 7.3 copy.84
  1071.5 99.7 %all_to_all.90 = s16[8,256,1024]{1,0,2:T(8,128)(2,1)} all-to-all(s16[8,256,1024]{1,0,2:T(8,128)(2,1)} %copy.84), channel_id=1, replica_groups=mesh['row'=4,'col'=4,'pt'=2] {'col'}, dimensions={2} | all-to-all | bytes 8388608 | tf_op jit(solution)/shard_map/all_to_all | solution.py:222
  1171.2 7.9 copy.86
  1179.1 4.5 copy.87
  1183.6 50.0 %all_to_all.91 = s16[32,256,256]{2,0,1:T(8,128)(2,1)S(1)} all-to-all(s16[32,256,256]{2,0,1:T(8,128)(2,1)S(1)} %copy.87), channel_id=1, replica_groups=mesh['row'=4,'col'=4,'pt'=2] {'pt'}, dimensions={1} | all-to-all | bytes 8388608 | tf_op jit(solution)/shard_map/all_to_all | solution.py:251
  1233.6 2.4 copy.88
  1236.0 1.4 convert_bitcast_fusion
  1237.4 4.9 copy.89
  1242.3 2.1 fusion.41
  1245.4 1.5 fusion.36
  1246.9 5.5 fusion.48
  1252.4 6.0 copy.90
  (38 shorter events, 9.6 us)
Async XLA Ops:
  0.0 5.5 copy-start.3
  0.0 6.8 copy-start.2
  6.7 1.4 copy-start.11
  19.6 100.0 %all-to-all-start = ((s16[32,256,256]{2,1,0:T(8,128)(2,1)}), s16[32,256,256]{2,1,0:T(8,128)(2,1)}, u32[]{:S(2)}, u32[]{:S(2)}) async-start(s16[32,256,256]{2,1,0:T(8,128)(2,1)} %copy.69), calls=%async_computation | async-start | bytes 8388608 | tf_op jit(solution)/shard_map/all_to_all | solution.py:213
  119.6 98.0 %all-to-all-start.1 = ((s16[32,256,256]{2,1,0:T(8,128)(2,1)}), s16[32,256,256]{2,1,0:T(8,128)(2,1)}, u32[]{:S(2)}, u32[]{:S(2)}) async-start(s16[32,256,256]{2,1,0:T(8,128)(2,1)} %copy.74), calls=%async_computation.1 | async-start | bytes 8388608 | tf_op jit(solution)/shard_map/all_to_all | solution.py:209
  416.3 12.5 copy-start.1
  416.3 12.5 copy-start.4
  423.6 99.2 %all-to-all-start.2 = ((s16[8,256,1024]{1,0,2:T(8,128)(2,1)}), s16[8,256,1024]{1,0,2:T(8,128)(2,1)}, u32[]{:S(2)}, u32[]{:S(2)}) async-start(s16[8,256,1024]{1,0,2:T(8,128)(2,1)} %copy.76), calls=%async_computation.2 | async-start | bytes 8388608 | tf_op jit(solution)/shard_map/all_to_all | solution.py:222
  539.8 4.5 copy-start.8
  544.3 1.3 copy-start.7
  545.5 1.5 copy-start.10
  648.0 9.1 copy-start
  671.3 97.4 %all-to-all-start.3 = ((s16[32,256,256]{2,1,0:T(8,128)(2,1)}), s16[32,256,256]{2,1,0:T(8,128)(2,1)}, u32[]{:S(2)}, u32[]{:S(2)}) async-start(s16[32,256,256]{2,1,0:T(8,128)(2,1)} %copy.78), calls=%async_computation.3 | async-start | bytes 8388608 | tf_op jit(solution)/shard_map/all_to_all | solution.py:213
  676.4 4.3 slice-start
  679.4 2.2 slice-start.1
  768.7 97.8 %all-to-all-start.4 = ((s16[32,256,256]{2,1,0:T(8,128)(2,1)}), s16[32,256,256]{2,1,0:T(8,128)(2,1)}, u32[]{:S(2)}, u32[]{:S(2)}) async-start(s16[32,256,256]{2,1,0:T(8,128)(2,1)} %copy.82), calls=%async_computation.4 | async-start | bytes 8388608 | tf_op jit(solution)/shard_map/all_to_all | solution.py:209
  1242.3 2.2 copy-start.5
  1244.4 1.0 copy-start.6
  1245.4 1.5 copy-start.9
